TPU v7x, 256 devices: a whole 4x4x8 slice. The times are simulated.
256 devices in a mesh: batch: 32 (over z, y_hi, core), seq: 8 (over x, y_lo).
Axes of the slice: x: 4, y: 4 (y_hi: 2, y_lo: 2; y = y_hi * 2 + y_lo), z: 8, core: 2. Of those that a mesh axis runs over, the one named last changes fastest.
Arguments:
- queries: bfloat16 [32768, 4096], P(('batch', 'seq')), parts along dimension 0, may hold values from -130 to 130
- span_keys: bfloat16 [32768, 1024], P(('batch', 'seq')), parts along dimension 0, may hold values from -6 to 6
- span_values: bfloat16 [32768, 1024], P(('batch', 'seq')), parts along dimension 0, may hold values from -6 to 6
- cache_keys: bfloat16 [131072, 1024], P(('batch', 'seq')), parts along dimension 0, may hold values from -6 to 6
- cache_values: bfloat16 [131072, 1024], P(('batch', 'seq')), parts along dimension 0, may hold values from -6 to 6
- span_start: int32 [32], P('batch'), parts along dimension 0, may hold values from 2048 to 16383, as said below
- prompt_length: int32 [32], P('batch'), parts along dimension 0, may hold values from 2304 to 17407, as said below
- window_size: int32 [32], P('batch'), parts along dimension 0, may hold values from 2048 to 4096
Outputs:
- attended: bfloat16 [32768, 4096], P(('batch', 'seq')), parts along dimension 0
There are 32 independent parts, one for each index of `batch`. A program takes and returns all parts, laid end to end along the dimension named above; each array names one. Nothing has to cross between parts.
Inputs may be any that keep to these rules, and one draw needn't show every extreme that they name: Cache row j holds position span_start - 4096 + j and is unused where that is negative. `prompt_length`: lies between span_start + 256 and span_start + 1024; block rows at or past it are padding.
All inputs are finite; a program needn't handle non-finite values.
Results may differ from a plain program's by a relative error of at most 0.0065.
Values may be sent and summed in bfloat16 or wider, within the bound.
No kernel may reach another device: no remote copies, remote signals or barrier semaphores. Data moves between devices by JAX's collectives and lax.ppermute only.
A program may use at most 128 MiB of HBM per device.

v0:
```python
import math

import jax
import jax.numpy as jnp
from jax import lax
from jax.experimental import pallas as pl
from jax.experimental.pallas import tpu as pltpu
from jax.sharding import PartitionSpec as P

NEG=-1e30
C=512
U=2
KT=0; HS=1
NC=5120//C
SCALE=(128**-0.5)*math.log2(math.e)
def attn_body(start_ref, plen_ref, win_ref, recv, out_ref, k_s, v_s, S0, S1, mx0, mx1, acc, tot):
    S=(S0,S1); mx=(mx0,mx1)
    for s in range(8):
        k_s[s*512:(s+1)*512]=recv[s,512:1024]
        v_s[s*512:(s+1)*512]=recv[s,1024:1536]
        k_s[4096+s*128:4224+s*128]=recv[s,1536:1664]
        v_s[4096+s*128:4224+s*128]=recv[s,1664:1792]
    start=start_ref[0]; live=plen_ref[0]-start; win=win_ref[0]
    kmin=jnp.maximum(4096-start,0)
    groups=jnp.minimum((live+127)//128,8)
    def low(s): return jnp.maximum(jnp.maximum(4096+s*128-win+1,kmin),0)
    def clo(s): return low(s)//C
    def chi(s): return (4096+s*128+127)//C
    def p1(s,b,c,masked):
        k=k_s[pl.ds(pl.multiple_of(c*C,C),C),:]
        R=512//HS
        if masked:
            i=lax.broadcasted_iota(jnp.int32,(128,C),0); kk=lax.broadcasted_iota(jnp.int32,(128,C),1)
            t=i-kk+(4096+s*128-c*C)
            ok=(t>=0)&(t<win)&(kk>=kmin-c*C)
        for h in range(HS):
            q=recv[s,h*R:(h+1)*R]
            sc=lax.dot_general(q,k,(((1,),(1,)),((),())),preferred_element_type=jnp.float32)
            if masked:
                sc=jnp.where(ok[None],sc.reshape(R//128,128,C),NEG).reshape(R,C)
            S[b][c,h*R:(h+1)*R]=sc
            m=sc[:,0:128]
            for j in range(1,C//128): m=jnp.maximum(m,sc[:,j*128:(j+1)*128])
            mx[b][h*R:(h+1)*R]=jnp.maximum(mx[b][h*R:(h+1)*R],m)
    def p2(b,c):
        v=v_s[pl.ds(pl.multiple_of(c*C,C),C),:]
        R=512//HS
        for h in range(HS):
            r=slice(h*R,(h+1)*R)
            m=mx[b][r]
            p=jnp.exp2((S[b][c,r]-jnp.tile(m,(1,C//128)))*SCALE)
            t=p[:,0:128]
            for j in range(1,C//128): t=t+p[:,j*128:(j+1)*128]
            tot[r]+=t
            acc[r]+=jnp.dot(p.astype(jnp.bfloat16),v,preferred_element_type=jnp.float32)
    def init(b): mx[b][...]=jnp.full((512,128),NEG,jnp.float32)
    def zero():
        acc[...]=jnp.zeros_like(acc); tot[...]=jnp.zeros_like(tot)
    def top(b): mx[b][...]=jnp.broadcast_to(jnp.max(mx[b][...],axis=1,keepdims=True),(512,128))
    def fin(s):
        o=acc[...]/jnp.sum(tot[...],axis=1,keepdims=True)
        i=lax.broadcasted_iota(jnp.int32,(4,128,128),1).reshape(512,128)
        out_ref[s]=jnp.where(i+s*128<live,o,0.0).astype(jnp.bfloat16)
    def loop(a,b,f): lax.fori_loop(a,b,lambda c,_:(f(c),0)[1],0)
    def stage(s1,s2,b1,b2):
        init(b1); zero()
        a,e1,e2=clo(s1),chi(s1),chi(s2)
        loop(clo(s2),a,lambda c:p2(b2,c))
        lo=jnp.maximum((low(s1)+127+C-1)//C,a)
        hi=jnp.minimum(e1,e2+1)
        def edge(j):
            c=jnp.where(j<lo,j,j-lo+hi)
            p1(s1,b1,c,True); p2(b2,c)
        loop(a,lo+e2+1-hi,edge)
        def inner(c):
            for u in range(U): p1(s1,b1,c+u,False)
            for u in range(U): p2(b2,c+u)
        n=(hi-lo)//U
        loop(0,n,lambda j:inner(lo+U*j))
        def rest(c):
            p1(s1,b1,c,False); p2(b2,c)
        loop(lo+n*U,hi,rest)
        loop(e2+1,e1+1,lambda c:p1(s1,b1,c,True))
        top(b1); fin(s2)
    init(0)
    loop(clo(0),chi(0)+1,lambda c:p1(0,0,c,True))
    top(0)
    def pair(u,_):
        t=2*u+1
        @pl.when(t<groups)
        def _(): stage(t,t-1,1,0)
        @pl.when(t+1<groups)
        def _(): stage(t+1,t,0,1)
        return 0
    lax.fori_loop(0,groups//2,pair,0)
    last=groups-1
    zero()
    @pl.when(lax.rem(last,2)==0)
    def _(): loop(clo(last),chi(last)+1,lambda c:p2(0,c))
    @pl.when(lax.rem(last,2)==1)
    def _(): loop(clo(last),chi(last)+1,lambda c:p2(1,c))
    fin(last)
    def dead(s): out_ref[s]=jnp.zeros((512,128),jnp.bfloat16)
    loop(groups,8,dead)

def attn(start,plen,win,recv):
    return pl.pallas_call(attn_body,
        out_shape=jax.ShapeDtypeStruct((8,512,128),jnp.bfloat16),
        in_specs=[pl.BlockSpec(memory_space=pltpu.SMEM)]*3+[pl.BlockSpec(memory_space=pltpu.VMEM)],
        out_specs=pl.BlockSpec(memory_space=pltpu.VMEM),
        scratch_shapes=[pltpu.VMEM((5120,128),jnp.bfloat16),pltpu.VMEM((5120,128),jnp.bfloat16),
            pltpu.VMEM((NC,512,C),jnp.float32),pltpu.VMEM((NC,512,C),jnp.float32),pltpu.VMEM((512,128),jnp.float32),pltpu.VMEM((512,128),jnp.float32),
            pltpu.VMEM((512,128),jnp.float32),pltpu.VMEM((512,128),jnp.float32)],
        compiler_params=pltpu.CompilerParams(vmem_limit_bytes=40<<20),
        cost_estimate=pl.CostEstimate(flops=2*2*4096*4352*128,bytes_accessed=5<<20,transcendentals=4096*4352),
        name="attend")(start,plen,win,recv)


def pack_body(q, sk, sv, ck, cv, out, qv, skv, svv, ckv, cvv, in_sems, sems):
    loads = [
        pltpu.make_async_copy(a, b, in_sems.at[i])
        for i, (a, b) in enumerate([(q, qv), (ck, ckv), (cv, cvv), (sk, skv), (sv, svv)])
    ]
    for c in loads:
        c.start()
    stores = []

    def cp(src, dst):
        c = pltpu.make_async_copy(src, dst, sems.at[len(stores)])
        c.start()
        stores.append(c)

    loads[0].wait()
    for e in range(8):
        for h in range(4):
            cp(qv.at[:, pl.ds((e * 4 + h) * 128, 128)], out.at[e, pl.ds(h * 128, 128)])
    for i, (v, at, count) in enumerate([(ckv, 512, 512), (cvv, 1024, 512), (skv, 1536, 128), (svv, 1664, 128)]):
        loads[1 + i].wait()
        for e in range(8):
            cp(v.at[:, pl.ds(e * 128, 128)], out.at[e, pl.ds(at, count)])
    for c in stores:
        c.wait()


def pack(*arrays):
    return pl.pallas_call(
        pack_body,
        out_shape=jax.ShapeDtypeStruct((8, 1792, 128), jnp.bfloat16),
        in_specs=[pl.BlockSpec(memory_space=pl.ANY)] * 5,
        out_specs=pl.BlockSpec(memory_space=pl.ANY),
        scratch_shapes=[pltpu.VMEM(a.shape, a.dtype) for a in arrays]
        + [pltpu.SemaphoreType.DMA((5,)), pltpu.SemaphoreType.DMA((64,))],
        compiler_params=pltpu.CompilerParams(vmem_limit_bytes=16 << 20),
        name="pack",
    )(*arrays)


def unpack_body(x, out):
    for s in range(x.shape[0]):
        for h in range(4):
            at = (s * 4 + h) * 128
            out[:, at : at + 128] = x[s, h * 128 : (h + 1) * 128]


def unpack(x):
    return pl.pallas_call(
        unpack_body,
        grid=(2,),
        out_shape=jax.ShapeDtypeStruct((128, 4096), jnp.bfloat16),
        in_specs=[pl.BlockSpec((4, 512, 128), lambda i: (i, 0, 0))],
        out_specs=pl.BlockSpec((128, 2048), lambda i: (0, i)),
        compiler_params=pltpu.CompilerParams(vmem_limit_bytes=16 << 20),
        name="unpack",
    )(x)


def body(queries, span_keys, span_values, cache_keys, cache_values, span_start, prompt_length, window_size):
    sent = pack(queries, span_keys, span_values, cache_keys, cache_values)
    got = lax.all_to_all(sent, "seq", split_axis=0, concat_axis=0, tiled=True)
    mixed = attn(span_start, prompt_length, window_size, got)
    back = lax.all_to_all(mixed, "seq", split_axis=0, concat_axis=0, tiled=True)
    return unpack(back)


def solution(mesh):
    rows = P(("batch", "seq"), None)
    placed = (rows,) * 5 + (P("batch"),) * 3
    return jax.shard_map(body, mesh=mesh, in_specs=placed, out_specs=rows, check_vma=False)
```

profile of v0, /device:TPU:32, one launch (start us, length us, event | category | flops | bytes accessed | tf_op | source)
XLA Modules:
  0.0 118.7 jit_solution(1174771885281480883)
XLA Ops:
  0.0 0.0 copy-start.1
  0.0 1.2 %copy-done.1 = bf16[128,4096]{1,0:T(8,128)(2,1)S(1)} copy-done((bf16[128,4096]{1,0:T(8,128)(2,1)S(1)}, bf16[128,4096]{1,0:T(8,128)(2,1)}, u32[]{:S(2)}) %copy-start.1) | copy-done | bytes 1048600
  1.2 0.0 copy-start.2
  1.2 1.2 %copy-done.2 = bf16[512,1024]{1,0:T(8,128)(2,1)S(1)} copy-done((bf16[512,1024]{1,0:T(8,128)(2,1)S(1)}, bf16[512,1024]{1,0:T(8,128)(2,1)}, u32[]{:S(2)}) %copy-start.2) | copy-done | bytes 1048600
  2.5 0.0 copy-start.3
  2.5 1.2 %copy-done.3 = bf16[512,1024]{1,0:T(8,128)(2,1)S(1)} copy-done((bf16[512,1024]{1,0:T(8,128)(2,1)S(1)}, bf16[512,1024]{1,0:T(8,128)(2,1)}, u32[]{:S(2)}) %copy-start.3) | copy-done | bytes 1048600
  3.7 0.0 copy-start.4
  3.7 0.9 copy-done.4
  4.6 0.0 copy-start.5
  4.6 0.9 copy-done.5
  5.6 1.9 %pack.1 = bf16[8,1792,128]{2,1,0:T(8,128)(2,1)S(1)} custom-call(bf16[128,4096]{1,0:T(8,128)(2,1)S(1)} %copy-done.1, bf16[128,1024]{1,0:T(8,128)(2,1)S(1)} %copy-done.4, bf16[128,1024]{1,0:T(8,128)(2,1)S(1)} %copy-done.5, bf16[512,1024]{1,0:T(8,128)(2,1)S(1)} %copy-done.2, bf16[512,1024]{1,0:T(8,128)(2,1)S(1)} %copy-done.3), custom_call_target="tpu_custom_call" | custom-call | tf_op jit(solution)/shard_map/pack/pallas_call | solution.py:146
  7.5 0.0 copy-start
  7.5 1.8 %copy-done = bf16[8,1792,128]{2,1,0:T(8,128)(2,1)} copy-done((bf16[8,1792,128]{2,1,0:T(8,128)(2,1)}, bf16[8,1792,128]{2,1,0:T(8,128)(2,1)S(1)}, u32[]{:S(2)}) %copy-start) | copy-done | bytes 3670040
  9.4 5.3 %all-to-all-start = ((bf16[8,1792,128]{2,1,0:T(8,128)(2,1)}), bf16[8,1792,128]{2,1,0:T(8,128)(2,1)}, u32[]{:S(2)}, u32[]{:S(2)}) async-start(bf16[8,1792,128]{2,1,0:T(8,128)(2,1)} %copy-done), calls=%async_computation | async-start | bytes 7340032 | tf_op jit(solution)/shard_map/all_to_all | solution.py:179
  16.6 50.6 %all-to-all-done.recv = bf16[8,1792,128]{2,1,0:T(8,128)(2,1)} async-done(((bf16[8,1792,128]{2,1,0:T(8,128)(2,1)}), bf16[8,1792,128]{2,1,0:T(8,128)(2,1)}, u32[]{:S(2)}, u32[]{:S(2)}) %all-to-all-start) | async-done | bytes 3670048 | tf_op jit(solution)/shard_map/all_to_all | solution.py:179
  67.3 36.5 %attend.1 = bf16[8,512,128]{2,1,0:T(8,128)(2,1)S(1)} custom-call(s32[1]{0:T(128)S(6)} %copy.9.start_ref, s32[1]{0:T(128)S(6)} %copy.10.plen_ref, s32[1]{0:T(128)S(6)} %copy.11.win_ref, bf16[8,1792,128]{2,1,0:T(8,128)(2,1)} %all-to-all-done.recv), custom_call_target="tpu_custom_call" | custom-call | flops 9126805504 | bytes 5242880 | tf_op jit(solution)/shard_map/attend/pallas_call | solution.py:107
  103.7 13.9 %all_to_all.10.x = bf16[8,512,128]{2,1,0:T(8,128)(2,1)S(1)} all-to-all(bf16[8,512,128]{2,1,0:T(8,128)(2,1)S(1)} %attend.1), channel_id=1, replica_groups=mesh['batch'=32,'seq'=8] {'seq'}, dimensions={0} | all-to-all | bytes 2097152 | tf_op jit(solution)/shard_map/all_to_all | solution.py:181
  117.6 1.1 unpack.1
Async XLA Ops:
  0.0 1.2 %copy-start.1 = (bf16[128,4096]{1,0:T(8,128)(2,1)S(1)}, bf16[128,4096]{1,0:T(8,128)(2,1)}, u32[]{:S(2)}) copy-start(bf16[128,4096]{1,0:T(8,128)(2,1)} %q.1) | copy-start | bytes 3145732
  1.2 1.2 %copy-start.2 = (bf16[512,1024]{1,0:T(8,128)(2,1)S(1)}, bf16[512,1024]{1,0:T(8,128)(2,1)}, u32[]{:S(2)}) copy-start(bf16[512,1024]{1,0:T(8,128)(2,1)} %ck.1) | copy-start | bytes 3145732
  2.5 1.2 %copy-start.3 = (bf16[512,1024]{1,0:T(8,128)(2,1)S(1)}, bf16[512,1024]{1,0:T(8,128)(2,1)}, u32[]{:S(2)}) copy-start(bf16[512,1024]{1,0:T(8,128)(2,1)} %cv.1) | copy-start | bytes 3145732
  3.7 0.9 copy-start.4
  4.6 0.9 copy-start.5
  7.5 1.8 %copy-start = (bf16[8,1792,128]{2,1,0:T(8,128)(2,1)}, bf16[8,1792,128]{2,1,0:T(8,128)(2,1)S(1)}, u32[]{:S(2)}) copy-start(bf16[8,1792,128]{2,1,0:T(8,128)(2,1)S(1)} %pack.1) | copy-start | bytes 11010052
  9.4 57.9 %all-to-all-start = ((bf16[8,1792,128]{2,1,0:T(8,128)(2,1)}), bf16[8,1792,128]{2,1,0:T(8,128)(2,1)}, u32[]{:S(2)}, u32[]{:S(2)}) async-start(bf16[8,1792,128]{2,1,0:T(8,128)(2,1)} %copy-done), calls=%async_computation | async-start | bytes 7340032 | tf_op jit(solution)/shard_map/all_to_all | solution.py:179
where the time goes:
time: 117 us; the launch traced here: 119 us
  waiting for transfers between devices  50.6 us (43%)
  Pallas kernels  39.5 us (34%)
  blocking collectives  13.9 us (12%)
  local copies, waits for them, and re-layouts  7.39 us (6%)
  starting transfers between devices  5.31 us (5%)
  between operations  1.98 us (2%)
    all_to_all x1, waiting for transfers between devices, body(): got = lax.all_to_all(sent, 'seq', split_axis=0, concat_axis=0, tiled=True)  50.6 us
    pallas_call x1, Pallas kernels, attn(): pl.pallas_call(attn_body, out_shape=jax.ShapeDtypeStruct((8, 512, 128), j...  36.5 us
    all_to_all x1, blocking collectives, body(): back = lax.all_to_all(mixed, 'seq', split_axis=0, concat_axis=0, tiled=True)  13.9 us
    unnamed x12, local copies, waits for them, and re-layouts  7.39 us
    all_to_all x1, starting transfers between devices, body(): got = lax.all_to_all(sent, 'seq', split_axis=0, concat_axis=0, tiled=True)  5.31 us
  transfers between devices with their start and end apart: 1, of which 1 were waited for; matrix products, arithmetic and copies ran while one was open for 0% of the time, Pallas kernels for 0%

commit v1 on v0

--- a/solution.py
+++ b/solution.py
@@ -10,55 +10,44 @@
 NEG=-1e30
 C=512
 U=2
-KT=0; HS=1
-NC=5120//C
+QT=0
 SCALE=(128**-0.5)*math.log2(math.e)
-def attn_body(start_ref, plen_ref, win_ref, recv, out_ref, k_s, v_s, S0, S1, mx0, mx1, acc, tot):
+def attn_body(start_ref, plen_ref, win_ref, recv, out_ref, k_s, v_s, q_s, S0, S1, mx0, mx1, acc, tot, sems):
     S=(S0,S1); mx=(mx0,mx1)
-    for s in range(8):
-        k_s[s*512:(s+1)*512]=recv[s,512:1024]
-        v_s[s*512:(s+1)*512]=recv[s,1024:1536]
-        k_s[4096+s*128:4224+s*128]=recv[s,1536:1664]
-        v_s[4096+s*128:4224+s*128]=recv[s,1664:1792]
     start=start_ref[0]; live=plen_ref[0]-start; win=win_ref[0]
     kmin=jnp.maximum(4096-start,0)
     groups=jnp.minimum((live+127)//128,8)
-    def low(s): return jnp.maximum(jnp.maximum(4096+s*128-win+1,kmin),0)
+    def low(s): return jnp.maximum(4096+s*128-win+1,kmin)
     def clo(s): return low(s)//C
     def chi(s): return (4096+s*128+127)//C
+    for s in range(8):
+        k_s[s*512:(s+1)*512]=recv[s,512:1024]
+        k_s[4096+s*128:4224+s*128]=recv[s,1536:1664]
+        v_s[s]=recv[s,1024:1536].T
+        v_s[8+s//4,:,(s%4)*128:(s%4+1)*128]=recv[s,1664:1792].T
+        if QT: q_s[s]=recv[s,0:512].T
     def p1(s,b,c,masked):
         k=k_s[pl.ds(pl.multiple_of(c*C,C),C),:]
-        R=512//HS
+        if QT: sc=jnp.dot(k,q_s[s],preferred_element_type=jnp.float32)
+        else: sc=lax.dot_general(k,recv[s,0:512],(((1,),(1,)),((),())),preferred_element_type=jnp.float32)
         if masked:
-            i=lax.broadcasted_iota(jnp.int32,(128,C),0); kk=lax.broadcasted_iota(jnp.int32,(128,C),1)
-            t=i-kk+(4096+s*128-c*C)
-            ok=(t>=0)&(t<win)&(kk>=kmin-c*C)
-        for h in range(HS):
-            q=recv[s,h*R:(h+1)*R]
-            sc=lax.dot_general(q,k,(((1,),(1,)),((),())),preferred_element_type=jnp.float32)
-            if masked:
-                sc=jnp.where(ok[None],sc.reshape(R//128,128,C),NEG).reshape(R,C)
-            S[b][c,h*R:(h+1)*R]=sc
-            m=sc[:,0:128]
-            for j in range(1,C//128): m=jnp.maximum(m,sc[:,j*128:(j+1)*128])
-            mx[b][h*R:(h+1)*R]=jnp.maximum(mx[b][h*R:(h+1)*R],m)
+            row=lax.broadcasted_iota(jnp.int32,(C,128),0); lane=lax.broadcasted_iota(jnp.int32,(C,128),1)
+            t=lane-row+(4096+s*128-c*C)
+            ok=(t>=0)&(t<win)&(row>=kmin-c*C)
+            sc=jnp.concatenate([jnp.where(ok,sc[:,h*128:(h+1)*128],NEG) for h in range(4)],1)
+        S[b][c]=sc
+        mx[b][...]=jnp.maximum(mx[b][...],jnp.max(sc.reshape(C//8,8,512),axis=0))
     def p2(b,c):
-        v=v_s[pl.ds(pl.multiple_of(c*C,C),C),:]
-        R=512//HS
-        for h in range(HS):
-            r=slice(h*R,(h+1)*R)
-            m=mx[b][r]
-            p=jnp.exp2((S[b][c,r]-jnp.tile(m,(1,C//128)))*SCALE)
-            t=p[:,0:128]
-            for j in range(1,C//128): t=t+p[:,j*128:(j+1)*128]
-            tot[r]+=t
-            acc[r]+=jnp.dot(p.astype(jnp.bfloat16),v,preferred_element_type=jnp.float32)
-    def init(b): mx[b][...]=jnp.full((512,128),NEG,jnp.float32)
+        p=jnp.exp2((S[b][c].reshape(C//8,8,512)-mx[b][...][None])*SCALE)
+        tot[...]+=jnp.sum(p,axis=0)
+        acc[...]+=jnp.dot(v_s[c],p.reshape(C,512).astype(jnp.bfloat16),preferred_element_type=jnp.float32)
+    def init(b): mx[b][...]=jnp.full((8,512),NEG,jnp.float32)
     def zero():
         acc[...]=jnp.zeros_like(acc); tot[...]=jnp.zeros_like(tot)
-    def top(b): mx[b][...]=jnp.broadcast_to(jnp.max(mx[b][...],axis=1,keepdims=True),(512,128))
+    def top(b): mx[b][...]=jnp.broadcast_to(jnp.max(mx[b][...],axis=0,keepdims=True),(8,512))
     def fin(s):
-        o=acc[...]/jnp.sum(tot[...],axis=1,keepdims=True)
+        o=acc[...]/jnp.sum(tot[...],axis=0,keepdims=True)
+        o=o.T
         i=lax.broadcasted_iota(jnp.int32,(4,128,128),1).reshape(512,128)
         out_ref[s]=jnp.where(i+s*128<live,o,0.0).astype(jnp.bfloat16)
     def loop(a,b,f): lax.fori_loop(a,b,lambda c,_:(f(c),0)[1],0)
@@ -108,9 +97,9 @@
         out_shape=jax.ShapeDtypeStruct((8,512,128),jnp.bfloat16),
         in_specs=[pl.BlockSpec(memory_space=pltpu.SMEM)]*3+[pl.BlockSpec(memory_space=pltpu.VMEM)],
         out_specs=pl.BlockSpec(memory_space=pltpu.VMEM),
-        scratch_shapes=[pltpu.VMEM((5120,128),jnp.bfloat16),pltpu.VMEM((5120,128),jnp.bfloat16),
-            pltpu.VMEM((NC,512,C),jnp.float32),pltpu.VMEM((NC,512,C),jnp.float32),pltpu.VMEM((512,128),jnp.float32),pltpu.VMEM((512,128),jnp.float32),
-            pltpu.VMEM((512,128),jnp.float32),pltpu.VMEM((512,128),jnp.float32)],
+        scratch_shapes=[pltpu.VMEM((5120,128),jnp.bfloat16),pltpu.VMEM((10,128,512),jnp.bfloat16),pltpu.VMEM((8,128,512),jnp.bfloat16),
+            pltpu.VMEM((10,512,C),jnp.float32),pltpu.VMEM((10,512,C),jnp.float32),pltpu.VMEM((8,512),jnp.float32),pltpu.VMEM((8,512),jnp.float32),
+            pltpu.VMEM((128,512),jnp.float32),pltpu.VMEM((8,512),jnp.float32),pltpu.SemaphoreType.DMA((40,))],
         compiler_params=pltpu.CompilerParams(vmem_limit_bytes=40<<20),
         cost_estimate=pl.CostEstimate(flops=2*2*4096*4352*128,bytes_accessed=5<<20,transcendentals=4096*4352),
         name="attend")(start,plen,win,recv)
@@ -150,7 +139,7 @@
         out_specs=pl.BlockSpec(memory_space=pl.ANY),
         scratch_shapes=[pltpu.VMEM(a.shape, a.dtype) for a in arrays]
         + [pltpu.SemaphoreType.DMA((5,)), pltpu.SemaphoreType.DMA((64,))],
-        compiler_params=pltpu.CompilerParams(vmem_limit_bytes=16 << 20),
+        compiler_params=pltpu.CompilerParams(vmem_limit_bytes=60 << 20),
         name="pack",
     )(*arrays)
 

time: 117 us -> 109 us (0.932)
  the two profiles are of different devices: /device:TPU:32 before, /device:TPU:64 now
where the time goes in v1:
time: 109 us; the launch traced here: 111 us
  waiting for transfers between devices  50.6 us (46%)
  Pallas kernels  39 us (36%)
  blocking collectives  14.2 us (13%)
  starting transfers between devices  5.32 us (5%)
  between operations  1.96 us (2%)
    all_to_all x1, waiting for transfers between devices, body(): got = lax.all_to_all(sent, 'seq', split_axis=0, concat_axis=0, tiled=True)  50.6 us
    pallas_call x1, Pallas kernels, attn(): pl.pallas_call(attn_body, out_shape=jax.ShapeDtypeStruct((8, 512, 128), j...  34.2 us
    all_to_all x1, blocking collectives, body(): back = lax.all_to_all(mixed, 'seq', split_axis=0, concat_axis=0, tiled=True)  14.2 us
    all_to_all x1, starting transfers between devices, body(): got = lax.all_to_all(sent, 'seq', split_axis=0, concat_axis=0, tiled=True)  5.32 us
    pallas_call x1, Pallas kernels, pack(): pl.pallas_call(pack_body, out_shape=jax.ShapeDtypeStruct((8, 1792, 128),...  3.66 us
  transfers between devices with their start and end apart: 1, of which 1 were waited for; matrix products, arithmetic and copies ran while one was open for 0% of the time, Pallas kernels for 0%

profile of v1, /device:TPU:64, one launch (start us, length us, event | category | flops | bytes accessed | tf_op | source)
XLA Modules:
  0.0 111.1 jit_solution(7534525456521344825)
XLA Ops:
  0.0 3.7 %pack.1 = bf16[8,1792,128]{2,1,0:T(8,128)(2,1)} custom-call(bf16[128,4096]{1,0:T(8,128)(2,1)} %q.1, bf16[128,1024]{1,0:T(8,128)(2,1)} %sk.1, bf16[128,1024]{1,0:T(8,128)(2,1)} %sv.1, bf16[512,1024]{1,0:T(8,128)(2,1)} %ck.1, bf16[512,1024]{1,0:T(8,128)(2,1)} %cv.1), custom_call_target="tpu_custom_call" | custom-call | tf_op jit(solution)/shard_map/pack/pallas_call | solution.py:135
  3.7 5.3 %all-to-all-start = ((bf16[8,1792,128]{2,1,0:T(8,128)(2,1)}), bf16[8,1792,128]{2,1,0:T(8,128)(2,1)}, u32[]{:S(2)}, u32[]{:S(2)}) async-start(bf16[8,1792,128]{2,1,0:T(8,128)(2,1)} %pack.1), calls=%async_computation | async-start | bytes 7340032 | tf_op jit(solution)/shard_map/all_to_all | solution.py:168
  10.9 50.6 %all-to-all-done.recv = bf16[8,1792,128]{2,1,0:T(8,128)(2,1)} async-done(((bf16[8,1792,128]{2,1,0:T(8,128)(2,1)}), bf16[8,1792,128]{2,1,0:T(8,128)(2,1)}, u32[]{:S(2)}, u32[]{:S(2)}) %all-to-all-start) | async-done | bytes 3670048 | tf_op jit(solution)/shard_map/all_to_all | solution.py:168
  61.6 34.2 %attend.1 = bf16[8,512,128]{2,1,0:T(8,128)(2,1)S(1)} custom-call(s32[1]{0:T(128)S(6)} %copy.9.start_ref, s32[1]{0:T(128)S(6)} %copy.10.plen_ref, s32[1]{0:T(128)S(6)} %copy.11.win_ref, bf16[8,1792,128]{2,1,0:T(8,128)(2,1)} %all-to-all-done.recv), custom_call_target="tpu_custom_call" | custom-call | flops 9126805504 | bytes 5242880 | tf_op jit(solution)/shard_map/attend/pallas_call | solution.py:96
  95.8 14.2 %all_to_all.10.x = bf16[8,512,128]{2,1,0:T(8,128)(2,1)S(1)} all-to-all(bf16[8,512,128]{2,1,0:T(8,128)(2,1)S(1)} %attend.1), channel_id=1, replica_groups=mesh['batch'=32,'seq'=8] {'seq'}, dimensions={0} | all-to-all | bytes 2097152 | tf_op jit(solution)/shard_map/all_to_all | solution.py:170
  110.0 1.1 unpack.1
Async XLA Ops:
  3.7 57.9 %all-to-all-start = ((bf16[8,1792,128]{2,1,0:T(8,128)(2,1)}), bf16[8,1792,128]{2,1,0:T(8,128)(2,1)}, u32[]{:S(2)}, u32[]{:S(2)}) async-start(bf16[8,1792,128]{2,1,0:T(8,128)(2,1)} %pack.1), calls=%async_computation | async-start | bytes 7340032 | tf_op jit(solution)/shard_map/all_to_all | solution.py:168

commit v2 on v1

--- a/solution.py
+++ b/solution.py
@@ -9,7 +9,8 @@
 
 NEG=-1e30
 C=512
-U=2
+U=4
+V=3
 QT=0
 SCALE=(128**-0.5)*math.log2(math.e)
 def attn_body(start_ref, plen_ref, win_ref, recv, out_ref, k_s, v_s, q_s, S0, S1, mx0, mx1, acc, tot, sems):
@@ -51,6 +52,16 @@
         i=lax.broadcasted_iota(jnp.int32,(4,128,128),1).reshape(512,128)
         out_ref[s]=jnp.where(i+s*128<live,o,0.0).astype(jnp.bfloat16)
     def loop(a,b,f): lax.fori_loop(a,b,lambda c,_:(f(c),0)[1],0)
+    def unrolled(a,e,f,n=U):
+        k=(e-a)//n
+        loop(0,k,lambda j:f(a+n*j,n))
+        if n>1: loop(a+n*k,e,lambda c:f(c,1))
+    def first(c,n):
+        for u in range(n): p1(0,0,c+u,True)
+    def final(b):
+        def f(c,n):
+            for u in range(n): p2(b,c+u)
+        return f
     def stage(s1,s2,b1,b2):
         init(b1); zero()
         a,e1,e2=clo(s1),chi(s1),chi(s2)
@@ -61,18 +72,16 @@
             c=jnp.where(j<lo,j,j-lo+hi)
             p1(s1,b1,c,True); p2(b2,c)
         loop(a,lo+e2+1-hi,edge)
-        def inner(c):
-            for u in range(U): p1(s1,b1,c+u,False)
-            for u in range(U): p2(b2,c+u)
+        def both(c,n):
+            for u in range(n):
+                p1(s1,b1,c+u,False); p2(b2,c+u)
         n=(hi-lo)//U
-        loop(0,n,lambda j:inner(lo+U*j))
-        def rest(c):
-            p1(s1,b1,c,False); p2(b2,c)
-        loop(lo+n*U,hi,rest)
+        loop(0,n,lambda j:both(lo+U*j,U))
+        unrolled(lo+n*U,hi,both,U//2)
         loop(e2+1,e1+1,lambda c:p1(s1,b1,c,True))
         top(b1); fin(s2)
     init(0)
-    loop(clo(0),chi(0)+1,lambda c:p1(0,0,c,True))
+    unrolled(clo(0),chi(0)+1,first,V)
     top(0)
     def pair(u,_):
         t=2*u+1
@@ -85,9 +94,9 @@
     last=groups-1
     zero()
     @pl.when(lax.rem(last,2)==0)
-    def _(): loop(clo(last),chi(last)+1,lambda c:p2(0,c))
+    def _(): unrolled(clo(last),chi(last)+1,final(0),V)
     @pl.when(lax.rem(last,2)==1)
-    def _(): loop(clo(last),chi(last)+1,lambda c:p2(1,c))
+    def _(): unrolled(clo(last),chi(last)+1,final(1),V)
     fin(last)
     def dead(s): out_ref[s]=jnp.zeros((512,128),jnp.bfloat16)
     loop(groups,8,dead)

time: 109 us -> 104 us (0.954); the launches traced: 111 us -> 102 us
  Pallas kernels: 39 us -> 30.6 us
    pallas_call x1, Pallas kernels: 34.2 us -> 25.9 us  [attn(): pl.pallas_call(attn_body, out_shape=jax.ShapeDtypeStruct((8, 512, 128), j...]
where the time goes in v2:
time: 104 us; the launch traced here: 102 us
  waiting for transfers between devices  50.6 us (49%)
  Pallas kernels  30.6 us (29%)
  blocking collectives  13.9 us (13%)
  starting transfers between devices  5.32 us (5%)
  between operations  1.96 us (2%)
    all_to_all x1, waiting for transfers between devices, body(): got = lax.all_to_all(sent, 'seq', split_axis=0, concat_axis=0, tiled=True)  50.6 us
    pallas_call x1, Pallas kernels, attn(): pl.pallas_call(attn_body, out_shape=jax.ShapeDtypeStruct((8, 512, 128), j...  25.9 us
    all_to_all x1, blocking collectives, body(): back = lax.all_to_all(mixed, 'seq', split_axis=0, concat_axis=0, tiled=True)  13.9 us
    all_to_all x1, starting transfers between devices, body(): got = lax.all_to_all(sent, 'seq', split_axis=0, concat_axis=0, tiled=True)  5.32 us
    pallas_call x1, Pallas kernels, pack(): pl.pallas_call(pack_body, out_shape=jax.ShapeDtypeStruct((8, 1792, 128),...  3.66 us
  transfers between devices with their start and end apart: 1, of which 1 were waited for; matrix products, arithmetic and copies ran while one was open for 0% of the time, Pallas kernels for 0%

profile of v2, /device:TPU:64, one launch (start us, length us, event | category | flops | bytes accessed | tf_op | source)
XLA Modules:
  0.0 102.4 jit_solution(5843413740926258076)
XLA Ops:
  0.0 3.7 %pack.1 = bf16[8,1792,128]{2,1,0:T(8,128)(2,1)} custom-call(bf16[128,4096]{1,0:T(8,128)(2,1)} %q.1, bf16[128,1024]{1,0:T(8,128)(2,1)} %sk.1, bf16[128,1024]{1,0:T(8,128)(2,1)} %sv.1, bf16[512,1024]{1,0:T(8,128)(2,1)} %ck.1, bf16[512,1024]{1,0:T(8,128)(2,1)} %cv.1), custom_call_target="tpu_custom_call" | custom-call | tf_op jit(solution)/shard_map/pack/pallas_call | solution.py:144
  3.7 5.3 %all-to-all-start = ((bf16[8,1792,128]{2,1,0:T(8,128)(2,1)}), bf16[8,1792,128]{2,1,0:T(8,128)(2,1)}, u32[]{:S(2)}, u32[]{:S(2)}) async-start(bf16[8,1792,128]{2,1,0:T(8,128)(2,1)} %pack.1), calls=%async_computation | async-start | bytes 7340032 | tf_op jit(solution)/shard_map/all_to_all | solution.py:177
  10.9 50.6 %all-to-all-done.recv = bf16[8,1792,128]{2,1,0:T(8,128)(2,1)} async-done(((bf16[8,1792,128]{2,1,0:T(8,128)(2,1)}), bf16[8,1792,128]{2,1,0:T(8,128)(2,1)}, u32[]{:S(2)}, u32[]{:S(2)}) %all-to-all-start) | async-done | bytes 3670048 | tf_op jit(solution)/shard_map/all_to_all | solution.py:177
  61.6 25.9 %attend.1 = bf16[8,512,128]{2,1,0:T(8,128)(2,1)S(1)} custom-call(s32[1]{0:T(128)S(6)} %copy.9.start_ref, s32[1]{0:T(128)S(6)} %copy.10.plen_ref, s32[1]{0:T(128)S(6)} %copy.11.win_ref, bf16[8,1792,128]{2,1,0:T(8,128)(2,1)} %all-to-all-done.recv), custom_call_target="tpu_custom_call" | custom-call | flops 9126805504 | bytes 5242880 | tf_op jit(solution)/shard_map/attend/pallas_call | solution.py:105
  87.4 13.9 %all_to_all.10.x = bf16[8,512,128]{2,1,0:T(8,128)(2,1)S(1)} all-to-all(bf16[8,512,128]{2,1,0:T(8,128)(2,1)S(1)} %attend.1), channel_id=1, replica_groups=mesh['batch'=32,'seq'=8] {'seq'}, dimensions={0} | all-to-all | bytes 2097152 | tf_op jit(solution)/shard_map/all_to_all | solution.py:179
  101.3 1.1 %unpack.1 = bf16[128,4096]{1,0:T(8,128)(2,1)} custom-call(bf16[8,512,128]{2,1,0:T(8,128)(2,1)S(1)} %all_to_all.10.x), custom_call_target="tpu_custom_call" | custom-call | tf_op jit(solution)/shard_map/unpack/pallas_call | solution.py:164
Async XLA Ops:
  3.7 57.9 %all-to-all-start = ((bf16[8,1792,128]{2,1,0:T(8,128)(2,1)}), bf16[8,1792,128]{2,1,0:T(8,128)(2,1)}, u32[]{:S(2)}, u32[]{:S(2)}) async-start(bf16[8,1792,128]{2,1,0:T(8,128)(2,1)} %pack.1), calls=%async_computation | async-start | bytes 7340032 | tf_op jit(solution)/shard_map/all_to_all | solution.py:177
